TPU v7x, 128 devices: a whole 4x4x4 slice. The times are simulated.
128 devices in a mesh: lat: 16 (over y, x), lev: 8 (over z, core).
Axes of the slice: x: 4, y: 4, z: 4, core: 2. Of those that a mesh axis runs over, the one named last changes fastest.
Arguments:
- fourier: bfloat16 [2560, 96, 1024], P('lat', 'lev'), may hold values from -6 to 6
- table: int32 [512], replicated, may hold values from 0 to 511, each once
- legendre: bfloat16 [512, 2, 513, 1280], P(('lat', 'lev')), may hold values from -0.15625 to 0.15625
Outputs:
- spectral: bfloat16 [512, 2, 96, 513], P(('lat', 'lev'))
Inputs may be any that keep to these rules, and one draw needn't show every extreme that they name: `table`: every pair index appears exactly once.
All inputs are finite; a program needn't handle non-finite values.
Results may differ from a plain program's by a relative error of at most 0.0051.
Values may be sent and summed in bfloat16 or wider, within the bound.
A program may use at most 128 MiB of HBM per device.

v0:
```python
import jax
import jax.numpy as jnp
from jax import lax
from jax.sharding import PartitionSpec as P


def partner_2(array, axis, apart):
    return lax.ppermute(array, axis, [(i, i ^ 1 << apart) for i in range(lax.axis_size(axis))])


def regroup(outgoing, lat_count, lev_count):
    lat_rows, channels, width = outgoing.shape
    devices = lat_count * lev_count
    shaped = outgoing.reshape((1, lat_rows, channels, devices, width // devices))
    arrived = lax.all_to_all(shaped, ("lat", "lev"), split_axis=3, concat_axis=0, tiled=True)
    return arrived.reshape((devices, lat_rows, channels, width // devices))


def on_device(fourier, table, legendre):
    lat_count = lax.axis_size("lat")
    lev_count = lax.axis_size("lev")
    half_lat = lat_count // 2
    lat_rows, channels, wavenumbers = fourier.shape
    slot_count = legendre.shape[0]
    degree_rows = legendre.shape[2]
    columns = jnp.stack([table, wavenumbers - 1 - table], axis=1).reshape(-1)
    picked = jnp.take(fourier, columns, axis=2)
    top_bit = lat_count.bit_length() - 2
    partner = partner_2(picked, "lat", top_bit)
    mirror_sign = jnp.where(lax.axis_index("lat") < half_lat, 1.0, -1.0).astype(jnp.float32)
    merged = (partner.astype(jnp.float32) + mirror_sign * picked.astype(jnp.float32)).astype(
        jnp.bfloat16
    )
    arrived = regroup(merged, lat_count, lev_count)
    halves = arrived.reshape(2, half_lat, lev_count, lat_rows, channels, slot_count, 2)
    tables = legendre.reshape(slot_count, 2, degree_rows, half_lat, lat_rows)
    products = jnp.einsum(
        "ealbcsw,serab->selcwr", halves, tables, preferred_element_type=jnp.float32
    )
    products = products.reshape(slot_count, 2, lev_count * channels, 2, degree_rows)
    position = lax.axis_index(("lat", "lev")) * slot_count
    owned = lax.dynamic_slice_in_dim(table, position, slot_count)
    parity = jnp.arange(2, dtype=jnp.int32)
    row_counts = (wavenumbers - owned[:, None] - parity[None, :] + 1) // 2
    first_member = jnp.arange(degree_rows, dtype=jnp.int32)[None, None, :] < row_counts[:, :, None]
    spectral = jnp.where(first_member[:, :, None, :], products[:, :, :, 0], products[:, :, :, 1])
    return spectral.astype(jnp.bfloat16)


def solution(mesh):
    in_specs = (P("lat", "lev", None), P(), P(("lat", "lev"), None, None, None))
    out_specs = P(("lat", "lev"), None, None, None)
    return jax.shard_map(
        on_device, mesh=mesh, in_specs=in_specs, out_specs=out_specs, check_vma=False
    )
```

profile of v0, /device:TPU:1, one launch (start us, length us, event | category | flops | bytes accessed | tf_op | source)
XLA Modules:
  0.0 261.4 jit_solution(3358809006206441309)
XLA Ops:
  0.0 0.7 broadcast_subtract_fusion
  0.7 0.7 pad_add_fusion
  1.4 0.1 copy.26
  1.5 0.2 reshape.91
  1.7 0.2 reshape.90
  1.9 13.0 %copy.28 = bf16[160,12,1024]{0,1,2:T(8,128)(2,1)} copy(bf16[160,12,1024]{2,0,1:T(8,128)(2,1)} %param.3) | data formatting | bytes 7864320 | tf_op args[0]
  14.9 13.0 %gather_fusion = bf16[1024,160,12]{1,2,0:T(8,128)(2,1)} fusion(bf16[160,12,1024]{0,1,2:T(8,128)(2,1)} %copy.28, s32[1024]{0:T(1024)S(1)} %broadcast_clamp_fusion), kind=kCustom, calls=%fused_computation | custom fusion | bytes 7868416 | tf_op jit(solution)/shard_map/jit(_take)/gather | solution.py:27
  28.0 10.5 %copy.29 = bf16[1024,160,12]{0,1,2:T(8,128)(2,1)} copy(bf16[1024,160,12]{1,2,0:T(8,128)(2,1)} %gather_fusion) | data formatting | bytes 7864320 | tf_op jit(solution)/shard_map/jit(_take)/gather | solution.py:27
  38.5 4.4 %select_bitcast_fusion = bf16[160,12,1024]{2,0,1:T(8,128)(2,1)} fusion(bf16[1024,160,12]{0,1,2:T(8,128)(2,1)} %copy.29, pred[1024]{0:T(1024)(128)(4,1)S(1)} %compare_and_fusion), kind=kLoop, calls=%fused_computation.4 | loop fusion | flops 1966080 | bytes 7865344 | tf_op jit(solution)/shard_map/jit(_take)/select_n | solution.py:27
  42.8 3.7 %collective-permute-start = (bf16[160,12,1024]{2,0,1:T(8,128)(2,1)}, bf16[160,12,1024]{2,0,1:T(8,128)(2,1)}, u32[]{:S(2)}, u32[]{:S(2)}) collective-permute-start(bf16[160,12,1024]{2,0,1:T(8,128)(2,1)} %select_bitcast_fusion), channel_id=1, source_target_pairs={{0,64},{8,72},{16,80},{24,88},{32,96},{40,104},{48,112},{56,120},{... | collective-permute-start | bytes 11796488 | tf_op jit(solution)/shard_map/ppermute | solution.py:8
  46.6 84.7 %collective-permute-done = bf16[160,12,1024]{2,0,1:T(8,128)(2,1)} collective-permute-done((bf16[160,12,1024]{2,0,1:T(8,128)(2,1)}, bf16[160,12,1024]{2,0,1:T(8,128)(2,1)}, u32[]{:S(2)}, u32[]{:S(2)}) %collective-permute-start) | collective-permute-done | bytes 3932192 | tf_op jit(solution)/shard_map/ppermute | solution.py:8
  131.3 7.3 %add_convert_fusion = bf16[160,12,1024]{2,0,1:T(8,128)(2,1)} fusion(bf16[160,12,1024]{2,0,1:T(8,128)(2,1)} %collective-permute-done, f32[]{:T(128)S(6)} %select_n.45, bf16[1024,160,12]{0,1,2:T(8,128)(2,1)} %copy.29, pred[1024]{0:T(1024)(128)(4,1)S(1)} %compare_and_fusion), kind=kLoop, calls=%fused_computation.1 | loop fusion | flops 11796480 | bytes 11797508 | tf_op jit(solution)/shard_map/convert_element_type | solution.py:31
  138.5 7.7 %copy.30 = bf16[160,12,1024]{0,2,1:T(8,128)(2,1)} copy(bf16[160,12,1024]{2,0,1:T(8,128)(2,1)} %add_convert_fusion) | data formatting | bytes 7864320 | tf_op jit(solution)/shard_map/convert_element_type | solution.py:31
  146.2 6.3 %copy.31 = bf16[1,160,12,128,8]{1,4,2,0,3:T(8,128)(2,1)} copy(bf16[1,160,12,128,8]{1,4,3,2,0:T(8,128)(2,1)} %bitcast.30) | data formatting | bytes 7864320 | tf_op jit(solution)/shard_map/reshape | solution.py:14
  152.5 12.0 %all-to-all-start = ((bf16[1,160,12,128,8]{1,4,2,0,3:T(8,128)(2,1)}), bf16[1,160,12,128,8]{1,4,2,0,3:T(8,128)(2,1)}, u32[]{:S(2)}, u32[]{:S(2)}) async-start(bf16[1,160,12,128,8]{1,4,2,0,3:T(8,128)(2,1)} %copy.31), calls=%async_computation | async-start | bytes 12582912 | tf_op jit(solution)/shard_map/all_to_all | solution.py:15
  164.5 27.1 %copy.33 = bf16[4,2,513,1280]{2,3,1,0:T(8,128)(2,1)} copy(bf16[4,2,513,1280]{3,1,2,0:T(2,128)(2,1)} %param.5) | data formatting | bytes 21012480 | tf_op args[2]
  191.6 0.8 dynamic-slice_subtract_fusion
  192.3 0.1 add_select_fusion
  192.4 0.1 iota_compare_fusion
  192.5 48.5 %all-to-all-done = bf16[1,160,12,128,8]{1,4,2,0,3:T(8,128)(2,1)} async-done(((bf16[1,160,12,128,8]{1,4,2,0,3:T(8,128)(2,1)}), bf16[1,160,12,128,8]{1,4,2,0,3:T(8,128)(2,1)}, u32[]{:S(2)}, u32[]{:S(2)}) %all-to-all-start) | async-done | bytes 3932192 | tf_op jit(solution)/shard_map/all_to_all | solution.py:15
  241.1 6.4 %copy.32 = bf16[1,160,12,128,8]{1,3,4,2,0:T(8,128)(2,1)S(1)} copy(bf16[1,160,12,128,8]{1,4,2,0,3:T(8,128)(2,1)} %all-to-all-done) | data formatting | bytes 7864320 | tf_op jit(solution)/shard_map/all_to_all | solution.py:15
  247.4 8.3 %fusion.2 = bf16[4,2,8,12,2,513]{5,2,4,3,1,0:T(8,128)(2,1)S(1)} fusion(bf16[4,2,513,8,160,1,1]{2,4,3,6,5,1,0:T(8,128)(2,1)} %bitcast.32, bf16[2,8,8,160,12,4,2]{3,2,1,0,6,5,4:T(8,128)(2,1)S(1)} %bitcast.33), kind=kOutput, calls=%fused_computation.5 | convolution fusion | flops 2017198080 | bytes 16014336 | tf_op jit(solution)/shard_map/ealbcsw,serab->selcwr/dot_general | solution.py:37
  255.7 1.6 copy.35
  257.3 2.8 %fusion.10 = (bf16[4,2,96,1,513]{4,3,2,1,0:T(2,128)(2,1)S(1)}, bf16[4,2,96,1,513]{4,3,2,1,0:T(2,128)(2,1)S(1)}) fusion(bf16[4,2,96,2,513]{4,3,2,1,0:T(2,128)(2,1)S(1)} %bitcast.31), kind=kLoop, calls=%fused_computation.26 | loop fusion | bytes 3151872 | tf_op jit(solution)/shard_map/slice | solution.py:46
  260.1 1.2 fusion.6
  (3 shorter events, 0.0 us)
Async XLA Ops:
  42.8 88.5 %collective-permute-start = (bf16[160,12,1024]{2,0,1:T(8,128)(2,1)}, bf16[160,12,1024]{2,0,1:T(8,128)(2,1)}, u32[]{:S(2)}, u32[]{:S(2)}) collective-permute-start(bf16[160,12,1024]{2,0,1:T(8,128)(2,1)} %select_bitcast_fusion), channel_id=1, source_target_pairs={{0,64},{8,72},{16,80},{24,88},{32,96},{40,104},{48,112},{56,120},{... | collective-permute-start | bytes 11796488 | tf_op jit(solution)/shard_map/ppermute | solution.py:8
  152.5 88.6 %all-to-all-start = ((bf16[1,160,12,128,8]{1,4,2,0,3:T(8,128)(2,1)}), bf16[1,160,12,128,8]{1,4,2,0,3:T(8,128)(2,1)}, u32[]{:S(2)}, u32[]{:S(2)}) async-start(bf16[1,160,12,128,8]{1,4,2,0,3:T(8,128)(2,1)} %copy.31), calls=%async_computation | async-start | bytes 12582912 | tf_op jit(solution)/shard_map/all_to_all | solution.py:15
where the time goes:
time: 263 us; the launch traced here: 261 us
  waiting for transfers between devices  133 us (51%)
  local copies, waits for them, and re-layouts  88.9 us (34%)
  starting transfers between devices  15.7 us (6%)
  other arithmetic  15.2 us (6%)
  matrix products  8.25 us (3%)
    ppermute x1, waiting for transfers between devices, partner_2(): lax.ppermute(array, axis, [(i, i ^ 1 << apart) for i in range(lax.axis_si...  84.7 us
    all_to_all x1, waiting for transfers between devices, regroup(): lax.all_to_all(shaped, ('lat', 'lev'), split_axis=3, concat_axis=0, tiled...  48.5 us
    unnamed x2, local copies, waits for them, and re-layouts  40.1 us
    gather x2, local copies, waits for them, and re-layouts, on_device(): picked = jnp.take(fourier, columns, axis=2)  23.5 us
    all_to_all x1, starting transfers between devices, regroup(): lax.all_to_all(shaped, ('lat', 'lev'), split_axis=3, concat_axis=0, tiled...  12 us
    dot_general x1, matrix products, on_device(): jnp.einsum('ealbcsw,serab->selcwr', halves, tables, preferred_element_typ...  8.25 us
    convert_element_type x1, local copies, waits for them, and re-layouts, on_device(): (partner.astype(jnp.float32) + mirror_sign * picked.astype(jnp.float32))....  7.7 us
    convert_element_type x1, other arithmetic, on_device(): (partner.astype(jnp.float32) + mirror_sign * picked.astype(jnp.float32))....  7.27 us
  transfers between devices with their start and end apart: 2, of which 2 were waited for; matrix products, arithmetic and copies ran while one was open for 11% of the time, Pallas kernels for 0%

commit v1 on v0

v1 whole, which is shorter than its diff:
```python
import functools

import jax
import jax.numpy as jnp
from jax import lax
from jax.experimental import pallas as pl
from jax.experimental.pallas import tpu as pltpu
from jax.sharding import PartitionSpec as P

MESH = pl.DeviceIdType.MESH
F32, BF16 = jnp.float32, jnp.bfloat16
SIDE = 4
LEVS = 8
DEVICES = 128
GROUPS = 4
RUN = DEVICES // GROUPS
ROWS = 8
ORDER = (2 | 8 | 32, 8, 16, 32, 64, 1, 4)
NT = (((1,), (1,)), ((), ()))


def hop(k):
    bits = 0
    for place, mask in enumerate(ORDER):
        bits = bits ^ (((k >> place) & 1) * mask)
    return bits & 3, (bits >> 2) & 3, (bits >> 4) & 3, (bits >> 6) & 1


def where_am_i():
    lat, lev = lax.axis_index("lat"), lax.axis_index("lev")
    return lat, lev, lat % SIDE, lat // SIDE


def target(k):
    lat, lev, x, y = where_am_i()
    dx, dy, dz, dc = hop(k)
    z, core = lev // 2, lev % 2
    return (y + dy) % SIDE * SIDE + (x + dx) % SIDE, (z + dz) % SIDE * 2 + (core + dc) % 2


def fused(
    table, fourier, legendre, spectral,
    rows_in, picks, outgoing, arrived, raw_tables, tables, spread, lanes, parts, totals,
    rows_sem, table_sem, send_sem, recv_sem, own_sem, plane_sem, all_sem,
):
    channels, lat_rows, width = fourier.shape
    slot_count, degree_rows = legendre.shape[0], legendre.shape[1]
    lat, lev, x, y = where_am_i()
    me = lat * LEVS + lev
    tail = lat_rows - 128
    fold = 128 // tail

    barrier = pltpu.get_barrier_semaphore()
    x_line = [(y * SIDE + (x + i) % SIDE, lev) for i in range(1, SIDE)]
    y_line = [((y + i) % SIDE * SIDE + x, lev) for i in range(1, SIDE)]
    z_line = [(lat, (lev + i) % LEVS) for i in range(1, LEVS)]
    for peer in x_line + y_line + z_line:
        pl.semaphore_signal(barrier, inc=1, device_id=peer, device_id_type=MESH)

    for c in range(channels):
        pltpu.make_async_copy(
            fourier.at[c, pl.ds(0, 128)], rows_in.at[pl.ds(c * 128, 128)], rows_sem
        ).start()
        pltpu.make_async_copy(
            fourier.at[c, pl.ds(128, tail)], rows_in.at[pl.ds(channels * 128 + c * tail, tail)], rows_sem
        ).start()
    for s in range(slot_count):
        pltpu.make_async_copy(legendre.at[s], raw_tables.at[s], table_sem.at[s]).start()

    sub = lax.broadcasted_iota(jnp.int32, (ROWS, width), 0)
    lane = lax.broadcasted_iota(jnp.int32, (ROWS, width), 1)

    def pick(k, carry):
        to_lat, to_lev = target(k)
        first = (to_lat * LEVS + to_lev) * slot_count
        pair = jnp.full((ROWS, width), table[first], jnp.int32)
        for s in range(1, slot_count):
            pair = jnp.where(sub // 2 == s, table[first + s], pair)
        column = jnp.where(sub % 2 == 0, pair, width - 1 - pair)
        picks[k] = jnp.where(lane == column, 1.0, 0.0).astype(BF16)
        return carry

    lax.fori_loop(0, DEVICES, pick, 0)
    pltpu.make_async_copy(rows_in, rows_in, rows_sem).wait()

    step = 384

    def gather(m):
        chosen = picks[pl.ds(m * RUN, RUN)].reshape(RUN * ROWS, width)

        def some(n, carry):
            at = pl.multiple_of(n * step, 128)
            got = lax.dot_general(
                chosen, rows_in[pl.ds(at, step), :], NT, preferred_element_type=F32
            )
            outgoing[pl.ds(m * RUN, RUN), :, pl.ds(at, step)] = got.astype(BF16).reshape(RUN, ROWS, step)
            return carry

        lax.fori_loop(0, channels * lat_rows // step, some, 0)

    gather(0)
    pl.semaphore_wait(barrier, len(x_line) + len(y_line) + len(z_line))
    for peer in y_line:
        pl.semaphore_signal(plane_sem, inc=1, device_id=peer, device_id_type=MESH)
    gather(1)
    pl.semaphore_wait(plane_sem, len(y_line))
    for peer in z_line:
        pl.semaphore_signal(all_sem, inc=1, device_id=peer, device_id_type=MESH)
    gather(2)
    gather(3)
    own = pltpu.make_async_copy(outgoing.at[0], arrived.at[me], own_sem)
    own.start()
    pl.semaphore_wait(all_sem, len(z_line))

    for m in range(GROUPS):
        def send(k, carry):
            pltpu.make_async_remote_copy(
                src_ref=outgoing.at[k],
                dst_ref=arrived.at[me],
                send_sem=send_sem,
                recv_sem=recv_sem.at[m],
                device_id=target(k),
                device_id_type=MESH,
            ).start()
            return carry

        lax.fori_loop(max(1, m * RUN), (m + 1) * RUN, send, 0)

    ri = lax.broadcasted_iota(jnp.int32, (256, 256), 0)
    ci = lax.broadcasted_iota(jnp.int32, (256, 256), 1)
    spread[...] = jnp.where(ci == ri % 128 * 2 + ri // 128, 1.0, 0.0).astype(BF16)
    source = jnp.where(ci < 128, ci, 128 + ci % tail)
    for q in range(fold):
        lanes[q] = jnp.where(ri == source + q * tail, 1.0, 0.0).astype(BF16)
    r_last = lax.broadcasted_iota(jnp.int32, (32, 256), 0)
    c_last = lax.broadcasted_iota(jnp.int32, (32, 256), 1)
    last = jnp.where((r_last % 16 == 0) & (c_last == 254 + r_last // 16), 1.0, 0.0).astype(BF16)

    def relay(s, start, chooser, at, count):
        raw = raw_tables[s, pl.ds(start, 128)].reshape(256, raw_tables.shape[3])
        apart = jnp.dot(chooser, raw, preferred_element_type=F32).astype(BF16)
        for a in range(LEVS):
            low = lat_rows * a // 128 * 128
            laid = jnp.dot(apart[:, low : low + 256], lanes[a % fold], preferred_element_type=F32).astype(BF16)
            g = a // SIDE * 2 + a % 2
            half = a % SIDE // 2
            for e in range(2):
                tables[g, s, e, pl.ds(at, count), half * 256 : half * 256 + 256] = laid[e * count : (e + 1) * count]

    for s in range(slot_count):
        pltpu.make_async_copy(legendre.at[s], raw_tables.at[s], table_sem.at[s]).wait()

        def block(j, carry):
            at = pl.multiple_of(j * 128, 128)
            relay(s, at, spread[...], at, 128)
            return carry

        lax.fori_loop(0, degree_rows // 128, block, 0)
        relay(s, degree_rows - 128, last, degree_rows - 1, 16)

    own.wait()
    lane8 = lax.broadcasted_iota(jnp.int32, (ROWS, 128), 1)
    for m in range(GROUPS):
        count = RUN - 1 if m == 0 else RUN
        some = arrived.at[pl.ds(0, count)]
        pltpu.make_async_copy(some, some, recv_sem.at[m]).wait()
        from_x, from_y = (x + m) % 2, (y + m // 2) % 2
        g = from_y * 2 + from_x
        for half in range(2):
            north = from_y * SIDE + from_x + 2 * half

            def fold_in(b, carry):
                upper = arrived[north * LEVS + b].astype(F32)
                lower = arrived[(north + 8) * LEVS + b].astype(F32)
                for e, both in enumerate((upper + lower, upper - lower)):
                    for c in range(channels):
                        at = pl.ds(pl.multiple_of((b * channels + c) * ROWS, ROWS), ROWS)
                        parts[half * 2, e, at, :] = both[:, c * 128 : c * 128 + 128]
                        rest = channels * 128 + c // fold * 128
                        parts[half * 2 + 1, e, at, :] = jnp.where(
                            lane8 // tail == c % fold, both[:, rest : rest + 128], 0.0
                        )
                return carry

            lax.fori_loop(0, LEVS, fold_in, 0)

        def multiply(n, carry):
            s, e = n // 2, n % 2
            left = jnp.concatenate(
                [
                    jnp.concatenate(
                        [
                            parts[i, e, pl.ds(2 * s + w, LEVS * channels, stride=ROWS), :].astype(BF16)
                            for i in range(4)
                        ],
                        axis=1,
                    )
                    for w in range(2)
                ],
                axis=0,
            )
            product = lax.dot_general(left, tables[g, s, e], NT, preferred_element_type=F32)
            if m == 0:
                totals[s, e] = product
            elif m < GROUPS - 1:
                totals[s, e] += product
            else:
                product = totals[s, e] + product
                limit = (width - table[me * slot_count + s] - e + 1) // 2
                degree = lax.broadcasted_iota(jnp.int32, (LEVS * channels, product.shape[1]), 1)
                chosen = jnp.where(degree < limit, product[: LEVS * channels], product[LEVS * channels :])
                spectral[s, e] = chosen[:, :degree_rows].astype(BF16)
            return carry

        lax.fori_loop(0, 2 * slot_count, multiply, 0)

    sent = outgoing.at[pl.ds(0, DEVICES - 1)]
    pltpu.make_async_copy(sent, sent, send_sem).wait()


def on_device(fourier, table, legendre):
    lat_rows, channels, width = fourier.shape
    slot_count, _, degree_rows, half_lats = legendre.shape
    padded = (degree_rows + 15) // 16 * 16
    return pl.pallas_call(
        fused,
        out_shape=jax.ShapeDtypeStruct((slot_count, 2, LEVS * channels, degree_rows), BF16),
        in_specs=[
            pl.BlockSpec(memory_space=pltpu.SMEM),
            pl.BlockSpec(memory_space=pltpu.HBM),
            pl.BlockSpec(memory_space=pltpu.HBM),
        ],
        out_specs=pl.BlockSpec(memory_space=pltpu.VMEM),
        scratch_shapes=[
            pltpu.VMEM((channels * lat_rows, width), BF16),
            pltpu.VMEM((DEVICES, ROWS, width), BF16),
            pltpu.VMEM((DEVICES, ROWS, channels * lat_rows), BF16),
            pltpu.VMEM((DEVICES, ROWS, channels * lat_rows), BF16),
            pltpu.VMEM((slot_count, degree_rows, 2, half_lats), BF16),
            pltpu.VMEM((GROUPS, slot_count, 2, padded, 512), BF16),
            pltpu.VMEM((256, 256), BF16),
            pltpu.VMEM((4, 256, 256), BF16),
            pltpu.VMEM((4, 2, LEVS * channels * ROWS, 128), F32),
            pltpu.VMEM((slot_count, 2, 2 * LEVS * channels, padded), F32),
            pltpu.SemaphoreType.DMA,
            pltpu.SemaphoreType.DMA((slot_count,)),
            pltpu.SemaphoreType.DMA,
            pltpu.SemaphoreType.DMA((GROUPS,)),
            pltpu.SemaphoreType.DMA,
            pltpu.SemaphoreType.REGULAR,
            pltpu.SemaphoreType.REGULAR,
        ],
        compiler_params=pltpu.CompilerParams(
            collective_id=0, has_side_effects=True, vmem_limit_bytes=63 << 20
        ),
    )(table, fourier.transpose(1, 0, 2), legendre.transpose(0, 2, 1, 3))


def solution(mesh):
    in_specs = (P("lat", "lev", None), P(), P(("lat", "lev"), None, None, None))
    out_specs = P(("lat", "lev"), None, None, None)
    return jax.shard_map(
        on_device, mesh=mesh, in_specs=in_specs, out_specs=out_specs, check_vma=False
    )
```

time: 263 us -> 76 us (0.29)
  the two profiles are of different devices: /device:TPU:1 before, /device:TPU:27 now
where the time goes in v1:
time: 76 us; the launch traced here: 75.8 us
  Pallas kernels  73.6 us (97%)
  local copies, waits for them, and re-layouts  2.23 us (3%)
    pallas_call x1, Pallas kernels, on_device(): pl.pallas_call(fused, out_shape=jax.ShapeDtypeStruct((slot_count, 2, LEVS...  73.6 us
    unnamed x1, local copies, waits for them, and re-layouts  2.23 us

profile of v1, /device:TPU:27, one launch (start us, length us, event | category | flops | bytes accessed | tf_op | source)
XLA Modules:
  0.0 75.8 jit_solution(18137829107467916867)
XLA Ops:
  0.0 73.6 %shard_map.37 = bf16[4,2,96,513]{3,2,1,0:T(8,128)(2,1)} custom-call(s32[512]{0:T(512)} %table.1, bf16[12,160,1024]{2,1,0:T(8,128)(2,1)} %bitcast.3, bf16[4,513,2,1280]{3,2,1,0:T(2,128)(2,1)} %bitcast.2), custom_call_target="tpu_custom_call" | custom-call | tf_op jit(solution)/shard_map/pallas_call | solution.py:225
  73.6 2.2 %copy.5 = bf16[4,2,96,513]{3,2,1,0:T(8,128)(2,1)} copy(bf16[4,2,96,513]{3,2,1,0:T(8,128)(2,1)} %shard_map.37) | data formatting | bytes 1575936

commit v2 on v1

v2 whole, which is shorter than its diff:
```python
import functools

import jax
import jax.numpy as jnp
from jax import lax
from jax.experimental import pallas as pl
from jax.experimental.pallas import tpu as pltpu
from jax.sharding import PartitionSpec as P

MESH = pl.DeviceIdType.MESH
F32, BF16 = jnp.float32, jnp.bfloat16
SIDE = 4
LEVS = 8
DEVICES = 128
GROUPS = 4
RUN = DEVICES // GROUPS
ROWS = 8
ORDER = (2 | 8 | 32, 32, 8, 16, 64)
NT = (((1,), (1,)), ((), ()))


def hop(i):
    bits = 0
    for place, mask in enumerate(ORDER):
        bits ^= (i >> place & 1) * mask
    return bits & 2, bits >> 2 & 2, bits >> 4 & 3, bits >> 6


def targets(m):
    lat, lev = lax.axis_index("lat"), lax.axis_index("lev")
    x, y, z, core = lat % SIDE + m % 2, lat // SIDE + m // 2, lev // 2, lev % 2
    xs = {d: (x + d) % SIDE for d in (0, 2)}
    ys = {d: (y + d) % SIDE * SIDE for d in (0, 2)}
    zs = {d: (z + d) % SIDE * 2 for d in range(SIDE)}
    lats = {(dx, dy): ys[dy] + xs[dx] for dx in xs for dy in ys}
    levs = {(dz, dc): zs[dz] + (core + dc) % 2 for dz in zs for dc in range(2)}
    hops = [hop(i) for i in range(RUN)]
    return [(lats[dx, dy], levs[dz, dc]) for dx, dy, dz, dc in hops]


def fused(
    table, fourier, legendre, spectral,
    rows_in, picks, outgoing, arrived, raw_tables, tables, spread, lanes, last_rows, parts, totals, last_totals,
    rows_sem, table_sem, send_sem, recv_sem, own_sem, all_sem,
):
    channels, lat_rows, width = fourier.shape
    slot_count, degree_rows = legendre.shape[0], legendre.shape[1]
    lat, lev = lax.axis_index("lat"), lax.axis_index("lev")
    x, y = lat % SIDE, lat // SIDE
    me = lat * LEVS + lev
    tail = lat_rows - 128
    fold = 128 // tail

    near = targets(0)[1:]
    links = [targets(m)[0] for m in range(1, GROUPS)]
    back = [((y - m // 2) % SIDE * SIDE + (x - m % 2) % SIDE, lev) for m in range(1, GROUPS)]
    barrier = pltpu.get_barrier_semaphore()
    for peer in near + links:
        pl.semaphore_signal(barrier, inc=1, device_id=peer, device_id_type=MESH)

    step = 384
    pieces = channels * lat_rows // step

    def piece(i):
        return rows_in.at[pl.ds(pl.multiple_of(i * step, 128), step)]

    for c in range(channels):
        pltpu.make_async_copy(
            fourier.at[c, pl.ds(0, 128)], rows_in.at[pl.ds(c * 128, 128)], rows_sem.at[c * 128 // step]
        ).start()
    for c in range(channels):
        pltpu.make_async_copy(
            fourier.at[c, pl.ds(128, tail)],
            rows_in.at[pl.ds(channels * 128 + c * tail, tail)],
            rows_sem.at[pieces - 1],
        ).start()
    for s in range(slot_count):
        pltpu.make_async_copy(legendre.at[s], raw_tables.at[s], table_sem.at[s]).start()

    sub = lax.broadcasted_iota(jnp.int32, (ROWS, 128), 0)
    lane = lax.broadcasted_iota(jnp.int32, (ROWS, 128), 1)

    def choose(m):
        for i, (to_lat, to_lev) in enumerate(targets(m)):
            first = (to_lat * LEVS + to_lev) * slot_count
            pair = jnp.full((ROWS, 128), table[first], jnp.int32)
            for s in range(1, slot_count):
                pair = jnp.where(sub // 2 == s, table[first + s], pair)
            column = jnp.where(sub % 2 == 0, pair, width - 1 - pair) - lane
            for t in range(width // 128):
                picks[i, :, t * 128 : t * 128 + 128] = jnp.where(column == t * 128, 1.0, 0.0).astype(BF16)

    def gather(m):
        choose(m)

        def some(i, carry):
            if m == 0:
                pltpu.make_async_copy(piece(i), piece(i), rows_sem.at[i]).wait()
            got = lax.dot_general(
                picks[...].reshape(RUN * ROWS, width), piece(i)[...], NT, preferred_element_type=F32
            )
            at = pl.ds(pl.multiple_of(i * step, 128), step)
            outgoing[m * RUN : (m + 1) * RUN, :, at] = got.astype(BF16).reshape(RUN, ROWS, step)
            return carry

        lax.fori_loop(0, pieces, some, 0)

    def send(m):
        for i, peer in enumerate(targets(m)):
            if m == 0 and i == 0:
                continue
            pltpu.make_async_remote_copy(
                src_ref=outgoing.at[m * RUN + i],
                dst_ref=arrived.at[me],
                send_sem=send_sem,
                recv_sem=recv_sem.at[m],
                device_id=peer,
                device_id_type=MESH,
            ).start()

    gather(0)
    pl.semaphore_wait(barrier, len(near) + len(links))
    for peer in back:
        pl.semaphore_signal(all_sem, inc=1, device_id=peer, device_id_type=MESH)
    send(0)
    own = pltpu.make_async_copy(outgoing.at[0], arrived.at[me], own_sem)
    own.start()
    gather(1)
    pl.semaphore_wait(all_sem, len(links))
    gather(2)
    send(1)
    gather(3)
    send(2)

    ri = lax.broadcasted_iota(jnp.int32, (256, 256), 0)
    ci = lax.broadcasted_iota(jnp.int32, (256, 256), 1)
    spread[...] = jnp.where(ci == ri % 128 * 2 + ri // 128, 1.0, 0.0).astype(BF16)
    source = jnp.where(ri < 128, ri, 128 + ri % tail)
    for q in range(fold):
        lanes[q] = jnp.where(ci == source + q * tail, 1.0, 0.0).astype(BF16)
    r_last = lax.broadcasted_iota(jnp.int32, (16, 256), 0)
    c_last = lax.broadcasted_iota(jnp.int32, (16, 256), 1)
    last = jnp.where(c_last == 254 + r_last // 8, 1.0, 0.0).astype(BF16)

    def relay(s, start, chooser):
        raw = raw_tables[s, pl.ds(start, 128)].reshape(256, raw_tables.shape[3])
        apart = jnp.dot(chooser, raw, preferred_element_type=F32).astype(BF16)
        for a in range(LEVS):
            low = lat_rows * a // 128 * 128
            yield a // SIDE * 2 + a % 2, a % SIDE // 2 * 256, apart[:, low : low + 256], lanes[a % fold]

    for s in range(slot_count):
        pltpu.make_async_copy(legendre.at[s], raw_tables.at[s], table_sem.at[s]).wait()

        def block(j, carry):
            at = pl.multiple_of(j * 128, 128)
            for g, place, apart, layout in relay(s, at, spread[...]):
                laid = lax.dot_general(layout, apart, NT, preferred_element_type=F32).astype(BF16)
                for e in range(2):
                    tables[g, s, e, place : place + 256, pl.ds(at, 128)] = laid[:, e * 128 : e * 128 + 128]
            return carry

        lax.fori_loop(0, degree_rows // 128, block, 0)
        for g, place, apart, layout in relay(s, degree_rows - 128, last):
            laid = lax.dot_general(apart, layout, NT, preferred_element_type=F32)
            for e in range(2):
                last_rows[g, s, e, :, place : place + 256] = laid[e * 8 : e * 8 + 8]
        if s == 0:
            send(3)

    own.wait()
    lane8 = lax.broadcasted_iota(jnp.int32, (ROWS, 128), 1)
    for m in range(GROUPS):
        count = DEVICES // GROUPS - (1 if m == 0 else 0)
        some = arrived.at[pl.ds(0, count)]
        pltpu.make_async_copy(some, some, recv_sem.at[m]).wait()
        from_x, from_y = (x + m) % 2, (y + m // 2) % 2
        g = from_y * 2 + from_x
        for half in range(2):
            north = from_y * SIDE + from_x + 2 * half

            def fold_in(b, carry):
                upper = arrived[north * LEVS + b].astype(F32)
                lower = arrived[(north + 8) * LEVS + b].astype(F32)
                for e, both in enumerate((upper + lower, upper - lower)):
                    for c in range(channels):
                        at = pl.ds(pl.multiple_of((b * channels + c) * ROWS, ROWS), ROWS)
                        parts[half * 2, e, at, :] = both[:, c * 128 : c * 128 + 128]
                        rest = channels * 128 + c // fold * 128
                        parts[half * 2 + 1, e, at, :] = jnp.where(
                            lane8 // tail == c % fold, both[:, rest : rest + 128], 0.0
                        )
                return carry

            lax.fori_loop(0, LEVS, fold_in, 0)

        def multiply(n, carry):
            s, e = n // 2, n % 2
            sides = [
                [parts[i, e, pl.ds(2 * s + w, LEVS * channels, stride=ROWS), :] for i in range(4)] for w in range(2)
            ]
            left = jnp.concatenate([jnp.concatenate(side, axis=1) for side in sides], axis=0).astype(BF16)
            product = jnp.dot(left, tables[g, s, e], preferred_element_type=F32)
            tops = sum(sides[1][i] * last_rows[g, s, e, 0:1, i * 128 : i * 128 + 128] for i in range(4))
            if m > 0:
                product = totals[s, e] + product
                tops = last_totals[s, e] + tops
            if m < GROUPS - 1:
                totals[s, e] = product
                last_totals[s, e] = tops
            else:
                limit = (width - table[me * slot_count + s] - e + 1) // 2
                degree = lax.broadcasted_iota(jnp.int32, (LEVS * channels, product.shape[1]), 1)
                chosen = jnp.where(degree < limit, product[: LEVS * channels], product[LEVS * channels :])
                spectral[s, e, :, : degree_rows - 1] = chosen.astype(BF16)
                spectral[s, e, :, degree_rows - 1 :] = jnp.sum(tops, axis=1, keepdims=True).astype(BF16)
            return carry

        lax.fori_loop(0, 2 * slot_count, multiply, 0, unroll=2)

    sent = outgoing.at[pl.ds(0, DEVICES - 1)]
    pltpu.make_async_copy(sent, sent, send_sem).wait()


def on_device(fourier, table, legendre):
    lat_rows, channels, width = fourier.shape
    slot_count, _, degree_rows, half_lats = legendre.shape
    whole = degree_rows - 1
    return pl.pallas_call(
        fused,
        out_shape=jax.ShapeDtypeStruct((slot_count, 2, LEVS * channels, degree_rows), BF16),
        in_specs=[
            pl.BlockSpec(memory_space=pltpu.SMEM),
            pl.BlockSpec(memory_space=pltpu.HBM),
            pl.BlockSpec(memory_space=pltpu.HBM),
        ],
        out_specs=pl.BlockSpec(memory_space=pltpu.VMEM),
        scratch_shapes=[
            pltpu.VMEM((channels * lat_rows, width), BF16),
            pltpu.VMEM((RUN, ROWS, width), BF16),
            pltpu.VMEM((DEVICES, ROWS, channels * lat_rows), BF16),
            pltpu.VMEM((DEVICES, ROWS, channels * lat_rows), BF16),
            pltpu.VMEM((slot_count, degree_rows, 2, half_lats), BF16),
            pltpu.VMEM((GROUPS, slot_count, 2, 512, whole), BF16),
            pltpu.VMEM((256, 256), BF16),
            pltpu.VMEM((4, 256, 256), BF16),
            pltpu.VMEM((GROUPS, slot_count, 2, 8, 512), F32),
            pltpu.VMEM((4, 2, LEVS * channels * ROWS, 128), F32),
            pltpu.VMEM((slot_count, 2, 2 * LEVS * channels, whole), F32),
            pltpu.VMEM((slot_count, 2, LEVS * channels, 128), F32),
            pltpu.SemaphoreType.DMA((channels * lat_rows // 384,)),
            pltpu.SemaphoreType.DMA((slot_count,)),
            pltpu.SemaphoreType.DMA,
            pltpu.SemaphoreType.DMA((GROUPS,)),
            pltpu.SemaphoreType.DMA,
            pltpu.SemaphoreType.REGULAR,
        ],
        compiler_params=pltpu.CompilerParams(
            collective_id=0, has_side_effects=True, vmem_limit_bytes=63 << 20
        ),
    )(table, fourier.transpose(1, 0, 2), legendre.transpose(0, 2, 1, 3))


def solution(mesh):
    in_specs = (P("lat", "lev", None), P(), P(("lat", "lev"), None, None, None))
    out_specs = P(("lat", "lev"), None, None, None)
    return jax.shard_map(
        on_device, mesh=mesh, in_specs=in_specs, out_specs=out_specs, check_vma=False
    )
```

time: 76 us -> 63.5 us (0.84)
  the two profiles are of different devices: /device:TPU:27 before, /device:TPU:1 now
where the time goes in v2:
time: 63.5 us; the launch traced here: 63.4 us
  Pallas kernels  61.1 us (96%)
  local copies, waits for them, and re-layouts  2.23 us (4%)
    pallas_call x1, Pallas kernels, on_device(): pl.pallas_call(fused, out_shape=jax.ShapeDtypeStruct((slot_count, 2, LEVS...  61.1 us
    unnamed x1, local copies, waits for them, and re-layouts  2.23 us

profile of v2, /device:TPU:1, one launch (start us, length us, event | category | flops | bytes accessed | tf_op | source)
XLA Modules:
  0.0 63.4 jit_solution(9672844782515224677)
XLA Ops:
  0.0 61.1 %shard_map.37 = bf16[4,2,96,513]{3,2,1,0:T(8,128)(2,1)} custom-call(s32[512]{0:T(512)} %table.1, bf16[12,160,1024]{2,1,0:T(8,128)(2,1)} %bitcast.3, bf16[4,513,2,1280]{3,2,1,0:T(2,128)(2,1)} %bitcast.2), custom_call_target="tpu_custom_call" | custom-call | tf_op jit(solution)/shard_map/pallas_call | solution.py:229
  61.1 2.2 %copy.5 = bf16[4,2,96,513]{3,2,1,0:T(8,128)(2,1)} copy(bf16[4,2,96,513]{3,2,1,0:T(8,128)(2,1)} %shard_map.37) | data formatting | bytes 1575936

commit v3 on v2

--- a/solution.py
+++ b/solution.py
@@ -216,7 +216,7 @@
                 spectral[s, e, :, degree_rows - 1 :] = jnp.sum(tops, axis=1, keepdims=True).astype(BF16)
             return carry
 
-        lax.fori_loop(0, 2 * slot_count, multiply, 0, unroll=2)
+        lax.fori_loop(0, 2 * slot_count, multiply, 0, unroll=8 if m == GROUPS - 1 else 2)
 
     sent = outgoing.at[pl.ds(0, DEVICES - 1)]
     pltpu.make_async_copy(sent, sent, send_sem).wait()

time: 63.5 us -> 63.2 us (level)
  no operation moved by 1% of the time
where the time goes in v3:
time: 63.2 us; the launch traced here: 63 us
  Pallas kernels  60.8 us (96%)
  local copies, waits for them, and re-layouts  2.23 us (4%)
    pallas_call x1, Pallas kernels, on_device(): pl.pallas_call(fused, out_shape=jax.ShapeDtypeStruct((slot_count, 2, LEVS...  60.8 us
    unnamed x1, local copies, waits for them, and re-layouts  2.23 us

profile of v3, /device:TPU:1, one launch (start us, length us, event | category | flops | bytes accessed | tf_op | source)
XLA Modules:
  0.0 63.0 jit_solution(6726181471675395337)
XLA Ops:
  0.0 60.8 %shard_map.37 = bf16[4,2,96,513]{3,2,1,0:T(8,128)(2,1)} custom-call(s32[512]{0:T(512)} %table.1, bf16[12,160,1024]{2,1,0:T(8,128)(2,1)} %bitcast.3, bf16[4,513,2,1280]{3,2,1,0:T(2,128)(2,1)} %bitcast.2), custom_call_target="tpu_custom_call" | custom-call | tf_op jit(solution)/shard_map/pallas_call | solution.py:229
  60.8 2.2 %copy.5 = bf16[4,2,96,513]{3,2,1,0:T(8,128)(2,1)} copy(bf16[4,2,96,513]{3,2,1,0:T(8,128)(2,1)} %shard_map.37) | data formatting | bytes 1575936

commit v4 on v3

--- a/solution.py
+++ b/solution.py
@@ -216,7 +216,7 @@
                 spectral[s, e, :, degree_rows - 1 :] = jnp.sum(tops, axis=1, keepdims=True).astype(BF16)
             return carry
 
-        lax.fori_loop(0, 2 * slot_count, multiply, 0, unroll=8 if m == GROUPS - 1 else 2)
+        lax.fori_loop(0, 2 * slot_count, multiply, 0, unroll=8 if m >= GROUPS - 2 else 2)
 
     sent = outgoing.at[pl.ds(0, DEVICES - 1)]
     pltpu.make_async_copy(sent, sent, send_sem).wait()

time: 63.2 us -> 63.2 us (level)
  no operation moved by 1% of the time
where the time goes in v4:
time: 63.2 us; the launch traced here: 63 us
  Pallas kernels  60.8 us (96%)
  local copies, waits for them, and re-layouts  2.23 us (4%)
    pallas_call x1, Pallas kernels, on_device(): pl.pallas_call(fused, out_shape=jax.ShapeDtypeStruct((slot_count, 2, LEVS...  60.8 us
    unnamed x1, local copies, waits for them, and re-layouts  2.23 us

profile of v4, /device:TPU:1, one launch (start us, length us, event | category | flops | bytes accessed | tf_op | source)
XLA Modules:
  0.0 63.0 jit_solution(13666528482485539349)
XLA Ops:
  0.0 60.8 %shard_map.37 = bf16[4,2,96,513]{3,2,1,0:T(8,128)(2,1)} custom-call(s32[512]{0:T(512)} %table.1, bf16[12,160,1024]{2,1,0:T(8,128)(2,1)} %bitcast.3, bf16[4,513,2,1280]{3,2,1,0:T(2,128)(2,1)} %bitcast.2), custom_call_target="tpu_custom_call" | custom-call | tf_op jit(solution)/shard_map/pallas_call | solution.py:229
  60.8 2.2 %copy.5 = bf16[4,2,96,513]{3,2,1,0:T(8,128)(2,1)} copy(bf16[4,2,96,513]{3,2,1,0:T(8,128)(2,1)} %shard_map.37) | data formatting | bytes 1575936
